TPU v7x, 256 devices: a whole 4x4x8 slice. The times are simulated.
256 devices in a mesh: ctx: 16 (over z, y_hi), grp: 16 (over y_lo, x, core).
Axes of the slice: x: 4, y: 4 (y_hi: 2, y_lo: 2; y = y_hi * 2 + y_lo), z: 8, core: 2. Of those that a mesh axis runs over, the one named last changes fastest.
Arguments:
- q_latent: bfloat16 [4096, 1536], P('ctx'), may hold values from -210 to 210
- kv_latent: bfloat16 [4096, 576], P('ctx'), may hold values from -6 to 6
- kv_gain: float32 [512], replicated, may hold values from 0.1 to 1.9
- q_weight: bfloat16 [1536, 24576], P('ctx', 'grp'), may hold values from -0.15625 to 0.15625
- kv_weight: bfloat16 [512, 32768], P('ctx', 'grp'), may hold values from -0.25 to 0.25
- out_weight: bfloat16 [16384, 7168], P('grp', 'ctx'), may hold values from -0.0625 to 0.0625
- documents: int32 [4096], replicated, may hold values from 0 to 7, never falling along the last dimension, each value on 1 to 1024 neighbouring positions
Outputs:
- mixed: bfloat16 [4096, 7168], P('ctx', 'grp')
All inputs are finite; a program needn't handle non-finite values.
Results may differ from a plain program's by a relative error of at most 0.018.
Values may be sent and summed in bfloat16 or wider, within the bound.
A program may use at most 64 MiB of HBM per device.

v0:
```python
import jax
import jax.numpy as jnp
from jax import lax
from jax.sharding import Mesh
from jax.sharding import PartitionSpec as P

KL = 512
NOPE = 128
ROPE = 64
VDIM = 128
CTX = ("ctx_0", "ctx_1")
epsilon = 1e-06


def gather_axes(array, axes, dim):
    result = array
    for number in range(len(axes) - 1, -1, -1):
        result = lax.all_gather(result, axes[number], axis=dim, tiled=True)
    return result


def shifted(block, axis, distance):
    devices = range(lax.axis_size(axis))
    route = [(i - distance, i) for i in devices if i - distance in devices]
    return lax.ppermute(block, axis, route)


def joined_along(tiles, dim):
    lengths = list(tiles.shape[1:])
    lengths[dim] *= tiles.shape[0]
    return jnp.moveaxis(tiles, 0, dim).reshape(lengths)


def copy_for_each(array, axis):
    count = lax.axis_size(axis)
    return lax.all_to_all(
        jnp.broadcast_to(array[None], (count, *array.shape)), axis, 0, 0, tiled=True
    )


def gathered_copies(array, axis, dim):
    return joined_along(copy_for_each(array, axis), dim)


def in_blocks(array, dim, count):
    lengths = array.shape
    tiles = array.reshape(*lengths[:dim], count, lengths[dim] // count, *lengths[dim + 1 :])
    return jnp.moveaxis(tiles, dim, 0)


def summed_on_arrival(array, axis, dim):
    count = lax.axis_size(axis)
    tiles = lax.all_to_all(in_blocks(array, dim, count), axis, 0, 0, tiled=True)
    return jnp.sum(tiles.astype(jnp.float32), axis=0)


def rotate(inputs, positions):
    half_width = inputs.shape[-1] // 2
    inverse = 10000.0 ** (-2.0 * jnp.arange(half_width, dtype=jnp.float32) / inputs.shape[-1])
    angles = positions.astype(jnp.float32)[:, None] * inverse[None, :]
    shape = (angles.shape[0],) + (1,) * (inputs.ndim - 2) + (half_width,)
    cosine = jnp.cos(angles).reshape(shape)
    sine_part = jnp.sin(angles).reshape(shape)
    front_half = inputs[..., :half_width]
    back_half = inputs[..., half_width:]
    return jnp.concatenate(
        [front_half * cosine - back_half * sine_part, back_half * cosine + front_half * sine_part],
        axis=-1,
    )


def prepare(latent_block, positions, kv_gain):
    latent = latent_block[:, :KL].astype(jnp.float32)
    normed = (
        latent * lax.rsqrt(jnp.mean(latent * latent, axis=-1, keepdims=True) + epsilon) * kv_gain
    )
    key_rope = rotate(latent_block[:, KL:].astype(jnp.float32), positions).astype(jnp.bfloat16)
    return (normed.astype(jnp.bfloat16), key_rope)


def folder(left, weight_piece):
    return jnp.dot(left, weight_piece, preferred_element_type=jnp.float32)


def per_device(q_latent, kv_latent, kv_gain, q_weight, kv_weight, out_weight, documents):
    rows_dev = q_latent.shape[0]
    head_count = q_weight.shape[1] // (NOPE + ROPE)
    block_index = lax.axis_index(CTX)
    query_pos = block_index * rows_dev + jnp.arange(rows_dev, dtype=jnp.int32)
    prior_pos = query_pos - rows_dev
    query_full = folder(q_latent, gather_axes(q_weight, CTX, 0))
    query_full = query_full.reshape(rows_dev, head_count, NOPE + ROPE)
    query_nope = query_full[..., :NOPE].astype(jnp.bfloat16)
    query_rope = rotate(query_full[..., NOPE:], query_pos).astype(jnp.bfloat16)
    previous = shifted(kv_latent, CTX, 1)
    latent_block = jnp.concatenate([previous, kv_latent], axis=0)
    positions = jnp.concatenate([prior_pos, query_pos])
    normed, key_rope = prepare(latent_block, positions, kv_gain)
    key_value = folder(normed, gathered_copies(kv_weight, CTX, 0))
    key_value = key_value.astype(jnp.bfloat16)
    key_value = key_value.reshape(2 * rows_dev, head_count, NOPE + VDIM)
    key_nope = key_value[..., :NOPE]
    values = key_value[..., NOPE:]
    key_pos = jnp.concatenate([prior_pos, query_pos])
    query_docs = lax.dynamic_slice_in_dim(documents, block_index * rows_dev, rows_dev, 0)
    prior_docs = lax.dynamic_slice_in_dim(
        documents, jnp.maximum(block_index - 1, 0) * rows_dev, rows_dev, 0
    )
    key_docs = jnp.concatenate([prior_docs, query_docs])
    allowed = (
        (key_docs[None, :] == query_docs[:, None])
        & (key_pos[None, :] <= query_pos[:, None])
        & (key_pos[None, :] >= 0)
    )
    scale = (NOPE + ROPE) ** (-0.5)
    scores = jnp.einsum("qhd,khd->hqk", query_nope, key_nope, preferred_element_type=jnp.float32)
    scores = (
        scores + jnp.einsum("qhr,kr->hqk", query_rope, key_rope, preferred_element_type=jnp.float32)
    ) * scale
    scores = jnp.where(allowed[None], scores, -1e30)
    highest = jnp.max(scores, axis=-1, keepdims=True)
    weights = jnp.exp(scores - highest)
    probs = (weights / jnp.sum(weights, axis=-1, keepdims=True)).astype(jnp.bfloat16)
    attended = jnp.einsum("hqk,khv->qhv", probs, values, preferred_element_type=jnp.float32).astype(
        jnp.bfloat16
    )
    attended = attended.reshape(rows_dev, head_count * VDIM)
    partial_value = jnp.dot(
        attended,
        lax.all_gather(out_weight, CTX, axis=1, tiled=True),
        preferred_element_type=jnp.float32,
    )
    mixed = summed_on_arrival(partial_value.astype(jnp.bfloat16), "grp", 1).astype(jnp.bfloat16)
    return mixed


def solution(mesh):
    torus = Mesh(mesh.devices.reshape(8, 2, mesh.shape["grp"]), ("ctx_0", "ctx_1", "grp"))
    return jax.shard_map(
        per_device,
        mesh=torus,
        in_specs=(
            P(CTX, None),
            P(CTX, None),
            P(),
            P(CTX, "grp"),
            P(CTX, "grp"),
            P("grp", CTX),
            P(),
        ),
        out_specs=P(CTX, "grp"),
        check_vma=False,
    )
```

profile of v0, /device:TPU:1, one launch (start us, length us, event | category | flops | bytes accessed | tf_op | source)
XLA Modules:
  0.0 416.1 jit_solution(16607223282581625902)
XLA Ops:
  6.5 12.7 %all_gather.9 = bf16[192,1536]{1,0:T(8,128)(2,1)} all-gather(bf16[96,1536]{1,0:T(8,128)(2,1)} %param.10), channel_id=1, replica_groups=mesh['ctx_0'=8,'ctx_1'=2,'grp'=16] {'ctx_1'}, dimensions={0}, use_global_device_ids=true | all-gather | bytes 884736 | tf_op jit(solution)/shard_map/all_gather | solution.py:18
  20.0 2.5 broadcast_in_dim.10
  22.5 9.6 %all-to-all-start = ((bf16[16,32,2048]{2,1,0:T(8,128)(2,1)}), bf16[16,32,2048]{2,1,0:T(8,128)(2,1)S(1)}, u32[]{:S(2)}, u32[]{:S(2)}) async-start(bf16[16,32,2048]{2,1,0:T(8,128)(2,1)} %broadcast_in_dim.10), calls=%async_computation | async-start | bytes 4194304 | tf_op jit(solution)/shard_map/all_to_all | solution.py:36
  32.1 5.5 %collective-permute-start = (bf16[256,576]{0,1:T(8,128)(2,1)S(1)}, bf16[256,576]{0,1:T(8,128)(2,1)}, u32[]{:S(2)}, u32[]{:S(2)}) collective-permute-start(bf16[256,576]{0,1:T(8,128)(2,1)S(1)} %copy-done.3), channel_id=1, source_target_pairs={{0,16},{16,32},{32,48},{48,64},{64,80},{80,96},{96,112},{112,128},... | collective-permute-start | bytes 884744 | tf_op jit(solution)/shard_map/ppermute | solution.py:25
  37.6 0.8 fusion.34
  38.5 0.8 multiply_cosine_fusion.1
  39.3 0.8 and_and_fusion
  40.2 0.9 collective-permute-done
  41.0 1.0 constant_dynamic-update-slice_fusion.1
  42.0 1.0 constant_dynamic-update-slice_fusion
  43.5 59.8 %all-to-all-done = bf16[16,32,2048]{2,1,0:T(8,128)(2,1)S(1)} async-done(((bf16[16,32,2048]{2,1,0:T(8,128)(2,1)}), bf16[16,32,2048]{2,1,0:T(8,128)(2,1)S(1)}, u32[]{:S(2)}, u32[]{:S(2)}) %all-to-all-start) | async-done | bytes 2097184 | tf_op jit(solution)/shard_map/all_to_all | solution.py:36
  103.3 1.4 convolution_convert_fusion.1
  105.6 20.3 %all-gather.3.cloned.1.call-done = bf16[1536,1536]{1,0:T(8,128)(2,1)} async-done(((bf16[192,1536]{1,0:T(8,128)(2,1)}), bf16[1536,1536]{1,0:T(8,128)(2,1)}) %all-gather.3.cloned.1.call-update) | async-done | bytes 4718608 | tf_op jit(solution)/shard_map/all_gather | solution.py:18
  125.9 4.3 %fusion.36 = f32[256,1536]{0,1:T(8,128)S(1)} fusion(bf16[256,1536]{1,0:T(8,128)(2,1)S(1)} %copy-done, bf16[1536,1536]{1,0:T(8,128)(2,1)} %all-gather.3.cloned.1.call-done), kind=kOutput, calls=%fused_computation.60 | convolution fusion | flops 1207959552 | bytes 7077888 | tf_op jit(solution)/shard_map/dot_general | solution.py:82
  130.3 0.8 fusion.8
  131.1 1.0 fusion.2
  132.0 2.0 copy-done.1
  134.0 1.7 fusion.35
  135.8 7.5 %fusion.4 = bf16[8,128,256]{2,1,0:T(8,128)(2,1)S(1)} fusion(f32[8,256]{1,0:T(8,128)S(1)} %fusion.35, bf16[512,8,128]{2,1,0:T(8,128)(2,1)S(1)} %get-tuple-element.5, f32[8,256,512]{2,1,0:T(8,128)} %copy-done.1), kind=kOutput, calls=%fused_computation.11 | convolution fusion | flops 271845888 | bytes 5775360 | tf_op jit(solution)/shard_map/hqk,khv->qhv/dot_general | solution.py:124
  143.3 191.3 %all-gather.5.cloned.1.call-done = bf16[1024,7168]{0,1:T(8,128)(2,1)} async-done(((bf16[1024,448]{0,1:T(8,128)(2,1)}), bf16[1024,7168]{0,1:T(8,128)(2,1)}) %all-gather.5.cloned.1.call-update) | async-done | bytes 14680080 | tf_op jit(solution)/shard_map/all_gather | solution.py:130
  334.6 16.4 %convolution_convert_fusion = bf16[256,7168]{1,0:T(8,128)(2,1)} fusion(bf16[256,1024]{0,1:T(8,128)(2,1)S(1)} %bitcast.32, bf16[1024,7168]{0,1:T(8,128)(2,1)} %all-gather.5.cloned.1.call-done), kind=kOutput, calls=%fused_computation.1 | convolution fusion | flops 3759931392 | bytes 18874368 | tf_op jit(solution)/shard_map/dot_general | solution.py:128
  351.0 5.9 %copy.25 = bf16[256,7168]{0,1:T(8,128)(2,1)} copy(bf16[256,7168]{1,0:T(8,128)(2,1)} %convolution_convert_fusion) | data formatting | bytes 7340032 | tf_op jit(solution)/shard_map/convert_element_type | solution.py:133
  356.9 49.1 %all_to_all.10 = bf16[16,256,448]{1,2,0:T(8,128)(2,1)} all-to-all(bf16[16,256,448]{1,2,0:T(8,128)(2,1)} %bitcast.26), channel_id=1, replica_groups=mesh['ctx_0'=8,'ctx_1'=2,'grp'=16] {'grp'}, dimensions={0} | all-to-all | bytes 7340032 | tf_op jit(solution)/shard_map/all_to_all | solution.py:53
  406.0 3.3 reduce_sum.32
  (30 shorter events, 2.2 us)
Async XLA Ops:
  6.5 119.3 %copy-start = (bf16[256,1536]{1,0:T(8,128)(2,1)S(1)}, bf16[256,1536]{1,0:T(8,128)(2,1)}, u32[]{:S(2)}) copy-start(bf16[256,1536]{1,0:T(8,128)(2,1)} %param.7) | copy-start | bytes 2359300
  6.5 25.5 %copy-start.3 = (bf16[256,576]{0,1:T(8,128)(2,1)S(1)}, bf16[256,576]{0,1:T(8,128)(2,1)}, u32[]{:S(2)}) copy-start(bf16[256,576]{0,1:T(8,128)(2,1)} %param.8) | copy-start | bytes 884740
  6.5 119.3 %all-gather.3.cloned.1.call-start = ((), (), s32[]{:S(2)}) async-start(), calls=%async_computation.2 | async-start | bytes 5308416 | tf_op jit(solution)/shard_map/all_gather | solution.py:18
  19.3 315.3 %all-gather.5.cloned.1.call-start = ((), (), s32[]{:S(2)}) async-start(), calls=%async_computation.3 | async-start | bytes 15597568 | tf_op jit(solution)/shard_map/all_gather | solution.py:130
  20.0 83.3 %copy-start.6 = (f32[512]{0:T(512)S(1)}, f32[512]{0:T(512)}, u32[]{:S(2)}) copy-start(f32[512]{0:T(512)} %param.9) | copy-start | bytes 6148
  22.5 80.8 %all-to-all-start = ((bf16[16,32,2048]{2,1,0:T(8,128)(2,1)}), bf16[16,32,2048]{2,1,0:T(8,128)(2,1)S(1)}, u32[]{:S(2)}, u32[]{:S(2)}) async-start(bf16[16,32,2048]{2,1,0:T(8,128)(2,1)} %broadcast_in_dim.10), calls=%async_computation | async-start | bytes 4194304 | tf_op jit(solution)/shard_map/all_to_all | solution.py:36
  32.1 9.0 %collective-permute-start = (bf16[256,576]{0,1:T(8,128)(2,1)S(1)}, bf16[256,576]{0,1:T(8,128)(2,1)}, u32[]{:S(2)}, u32[]{:S(2)}) collective-permute-start(bf16[256,576]{0,1:T(8,128)(2,1)S(1)} %copy-done.3), channel_id=1, source_target_pairs={{0,16},{16,32},{32,48},{48,64},{64,80},{80,96},{96,112},{112,128},... | collective-permute-start | bytes 884744 | tf_op jit(solution)/shard_map/ppermute | solution.py:25
  105.5 24.6 %copy-start.4 = (f32[256,32]{0,1:T(8,128)S(1)}, f32[256,32]{0,1:T(8,128)}, u32[]{:S(2)}) copy-start(f32[256,32]{0,1:T(8,128)} %get-tuple-element.15) | copy-start | bytes 98308
  105.6 24.6 %copy-start.5 = (f32[256,32]{0,1:T(8,128)S(1)}, f32[256,32]{0,1:T(8,128)}, u32[]{:S(2)}) copy-start(f32[256,32]{0,1:T(8,128)} %get-tuple-element.16) | copy-start | bytes 98308
  130.2 0.9 copy-start.2
  132.0 2.0 copy-start.1
Sparse Core Ops, SparseCore 0:
  19.4 106.4 all-gather.2
  128.5 206.0 all-gather.4
where the time goes:
time: 417 us; the launch traced here: 416 us
  waiting for transfers between devices  273 us (65%)
  blocking collectives  61.8 us (15%)
  matrix products  31.3 us (8%)
  starting transfers between devices  15.1 us (4%)
  local copies, waits for them, and re-layouts  14.1 us (3%)
  between operations  13.6 us (3%)
  other arithmetic  7.32 us (2%)
    all_gather x1, waiting for transfers between devices, per_device(): lax.all_gather(out_weight, CTX, axis=1, tiled=True)  191 us
    all_to_all x1, waiting for transfers between devices, copy_for_each(): lax.all_to_all(jnp.broadcast_to(array[None], (count, *array.shape)), axis...  59.8 us
    all_to_all x1, blocking collectives, summed_on_arrival(): tiles = lax.all_to_all(in_blocks(array, dim, count), axis, 0, 0, tiled=True)  49.1 us
    all_gather x1, waiting for transfers between devices, gather_axes(): result = lax.all_gather(result, axes[number], axis=dim, tiled=True)  20.3 us
    dot_general x1, matrix products, per_device(): jnp.dot(attended, lax.all_gather(out_weight, CTX, axis=1, tiled=True), pr...  16.4 us
    all_gather x1, blocking collectives, gather_axes(): result = lax.all_gather(result, axes[number], axis=dim, tiled=True)  12.7 us
    all_to_all x1, starting transfers between devices, copy_for_each(): lax.all_to_all(jnp.broadcast_to(array[None], (count, *array.shape)), axis...  9.55 us
  transfers between devices with their start and end apart: 4, of which 4 were waited for; matrix products, arithmetic and copies ran while one was open for 6% of the time, Pallas kernels for 0%

commit v1 on v0

--- a/solution.py
+++ b/solution.py
@@ -10,6 +10,11 @@
 VDIM = 128
 CTX = ("ctx_0", "ctx_1")
 epsilon = 1e-06
+
+
+def swapped_in(block, name, dim):
+    repeated = jnp.stack([block] * lax.axis_size(name))
+    return jnp.concatenate(lax.all_to_all(repeated, name, 0, 0), axis=dim)
 
 
 def gather_axes(array, axes, dim):
@@ -126,9 +131,7 @@
     )
     attended = attended.reshape(rows_dev, head_count * VDIM)
     partial_value = jnp.dot(
-        attended,
-        lax.all_gather(out_weight, CTX, axis=1, tiled=True),
-        preferred_element_type=jnp.float32,
+        attended, swapped_in(out_weight, CTX, 1), preferred_element_type=jnp.float32
     )
     mixed = summed_on_arrival(partial_value.astype(jnp.bfloat16), "grp", 1).astype(jnp.bfloat16)
     return mixed

time: 417 us -> 571 us (1.37)
  the two profiles are of different devices: /device:TPU:1 before, /device:TPU:96 now
where the time goes in v1:
time: 571 us; the launch traced here: 570 us
  waiting for transfers between devices  352 us (62%)
  blocking collectives  138 us (24%)
  matrix products  31.5 us (6%)
  local copies, waits for them, and re-layouts  20 us (4%)
  between operations  13.6 us (2%)
  starting transfers between devices  9.77 us (2%)
  other arithmetic  6.02 us (1%)
    ppermute x1, waiting for transfers between devices, shifted(): return lax.ppermute(block, axis, route)  352 us
    all_to_all x1, blocking collectives, copy_for_each(): lax.all_to_all(jnp.broadcast_to(array[None], (count, *array.shape)), axis...  60.4 us
    all_to_all x1, blocking collectives, summed_on_arrival(): tiles = lax.all_to_all(in_blocks(array, dim, count), axis, 0, 0, tiled=True)  49.3 us
    all_gather x1, blocking collectives, gather_axes(): result = lax.all_gather(result, axes[number], axis=dim, tiled=True)  27.8 us
    dot_general x1, matrix products, per_device(): jnp.dot(attended, swapped_in(out_weight, CTX, 1), preferred_element_type=...  16.6 us
  transfers between devices with their start and end apart: 3, of which 1 were waited for; matrix products, arithmetic and copies ran while one was open for 4% of the time, Pallas kernels for 0%

profile of v1, /device:TPU:96, one launch (start us, length us, event | category | flops | bytes accessed | tf_op | source)
XLA Modules:
  0.0 570.3 jit_solution(8171488648848373302)
XLA Ops:
  6.5 1.2 broadcast_in_dim.10
  7.8 60.4 %all_to_all.15 = bf16[16,32,2048]{2,1,0:T(8,128)(2,1)S(1)} all-to-all(bf16[16,32,2048]{2,1,0:T(8,128)(2,1)S(1)} %broadcast_in_dim.10), channel_id=1, replica_groups=mesh['ctx_0'=8,'ctx_1'=2,'grp'=16] {'ctx_0','ctx_1'}, dimensions={0} | all-to-all | bytes 4194304 | tf_op jit(solution)/shard_map/all_to_all | solution.py:41
  68.2 8.2 %stack.2 = bf16[16,1024,448]{1,2,0:T(8,128)(2,1)} broadcast(bf16[1024,448]{0,1:T(8,128)(2,1)} %param.12), dimensions={1,2} | broadcast | bytes 15597568 | tf_op jit(solution)/shard_map/stack | solution.py:16
  76.5 7.1 %all-to-all-start.1 = ((bf16[16,1024,448]{1,2,0:T(8,128)(2,1)}), bf16[16,1024,448]{1,2,0:T(8,128)(2,1)}, u32[]{:S(2)}, u32[]{:S(2)}) async-start(bf16[16,1024,448]{1,2,0:T(8,128)(2,1)} %stack.2), calls=%async_computation.1 | async-start | bytes 29360128 | tf_op jit(solution)/shard_map/all_to_all | solution.py:17
  83.6 27.8 %all_gather.6 = bf16[192,1536]{1,0:T(8,128)(2,1)} all-gather(bf16[96,1536]{1,0:T(8,128)(2,1)S(1)} %copy-done.3), channel_id=1, replica_groups=mesh['ctx_0'=8,'ctx_1'=2,'grp'=16] {'ctx_1'}, dimensions={0}, use_global_device_ids=true | all-gather | bytes 884736 | tf_op jit(solution)/shard_map/all_gather | solution.py:23
  111.4 2.7 collective-permute-start
  114.1 0.8 fusion.34
  115.0 0.2 multiply_cosine_fusion.1
  115.2 0.2 and_and_fusion
  115.4 351.8 %collective-permute-done = bf16[256,576]{0,1:T(8,128)(2,1)} collective-permute-done((bf16[256,576]{0,1:T(8,128)(2,1)S(1)}, bf16[256,576]{0,1:T(8,128)(2,1)}, u32[]{:S(2)}, u32[]{:S(2)}) %collective-permute-start) | collective-permute-done | bytes 294944 | tf_op jit(solution)/shard_map/ppermute | solution.py:30
  467.2 1.0 constant_dynamic-update-slice_fusion.1
  468.4 0.3 fusion.23
  468.7 1.4 convolution_convert_fusion.1
  470.1 0.7 copy.32
  471.0 4.3 fusion.36
  475.4 0.8 fusion.8
  476.1 1.0 fusion.2
  477.1 1.9 copy-done.2
  479.0 1.7 fusion.35
  480.8 7.5 %fusion.4 = bf16[8,128,256]{2,1,0:T(8,128)(2,1)S(1)} fusion(f32[8,256]{1,0:T(8,128)S(1)} %fusion.35, bf16[512,8,128]{2,1,0:T(8,128)(2,1)S(1)} %get-tuple-element.5, f32[8,256,512]{2,1,0:T(8,128)} %copy-done.2), kind=kOutput, calls=%fused_computation.11 | convolution fusion | flops 271845888 | bytes 5775360 | tf_op jit(solution)/shard_map/hqk,khv->qhv/dot_general | solution.py:129
  488.3 16.6 %convolution_convert_fusion = bf16[256,7168]{1,0:T(8,128)(2,1)} fusion(bf16[256,1024]{0,1:T(8,128)(2,1)S(1)} %bitcast.35, bf16[1024,7168]{0,1:T(8,128)(2,1)} %bitcast.7), kind=kOutput, calls=%fused_computation.1 | convolution fusion | flops 3759931392 | bytes 18874368 | tf_op jit(solution)/shard_map/dot_general | solution.py:133
  504.9 5.9 %copy.26 = bf16[256,7168]{0,1:T(8,128)(2,1)} copy(bf16[256,7168]{1,0:T(8,128)(2,1)} %convolution_convert_fusion) | data formatting | bytes 7340032 | tf_op jit(solution)/shard_map/convert_element_type | solution.py:136
  510.8 49.3 %all_to_all.16 = bf16[16,256,448]{1,2,0:T(8,128)(2,1)} all-to-all(bf16[16,256,448]{1,2,0:T(8,128)(2,1)} %bitcast.29), channel_id=1, replica_groups=mesh['ctx_0'=8,'ctx_1'=2,'grp'=16] {'grp'}, dimensions={0} | all-to-all | bytes 7340032 | tf_op jit(solution)/shard_map/all_to_all | solution.py:58
  560.1 3.3 reduce_sum.32
  (27 shorter events, 0.5 us)
Async XLA Ops:
  6.5 464.4 %copy-start = (bf16[256,1536]{1,0:T(8,128)(2,1)S(1)}, bf16[256,1536]{1,0:T(8,128)(2,1)}, u32[]{:S(2)}) copy-start(bf16[256,1536]{1,0:T(8,128)(2,1)} %param.7) | copy-start | bytes 2359300
  76.5 7.1 %copy-start.3 = (bf16[96,1536]{1,0:T(8,128)(2,1)S(1)}, bf16[96,1536]{1,0:T(8,128)(2,1)}, u32[]{:S(2)}) copy-start(bf16[96,1536]{1,0:T(8,128)(2,1)} %param.10) | copy-start | bytes 884740
  76.5 34.9 %copy-start.4 = (bf16[256,576]{0,1:T(8,128)(2,1)S(1)}, bf16[256,576]{0,1:T(8,128)(2,1)}, u32[]{:S(2)}) copy-start(bf16[256,576]{0,1:T(8,128)(2,1)} %param.8) | copy-start | bytes 884740
  76.5 392.3 %copy-start.5 = (f32[512]{0:T(512)S(1)}, f32[512]{0:T(512)}, u32[]{:S(2)}) copy-start(f32[512]{0:T(512)} %param.9) | copy-start | bytes 6148
  76.5 411.9 %all-to-all-start.1 = ((bf16[16,1024,448]{1,2,0:T(8,128)(2,1)}), bf16[16,1024,448]{1,2,0:T(8,128)(2,1)}, u32[]{:S(2)}, u32[]{:S(2)}) async-start(bf16[16,1024,448]{1,2,0:T(8,128)(2,1)} %stack.2), calls=%async_computation.1 | async-start | bytes 29360128 | tf_op jit(solution)/shard_map/all_to_all | solution.py:17
  83.5 387.5 %all-gather.2.cloned.1.call-start = ((), (), s32[]{:S(2)}) async-start(), calls=%async_computation.3 | async-start | bytes 5308416 | tf_op jit(solution)/shard_map/all_gather | solution.py:23
  111.4 355.8 %collective-permute-start = (bf16[256,576]{0,1:T(8,128)(2,1)S(1)}, bf16[256,576]{0,1:T(8,128)(2,1)}, u32[]{:S(2)}, u32[]{:S(2)}) collective-permute-start(bf16[256,576]{0,1:T(8,128)(2,1)S(1)} %copy-done.4), channel_id=1, source_target_pairs={{0,16},{16,32},{32,48},{48,64},{64,80},{80,96},{96,112},{112,128},... | collective-permute-start | bytes 884744 | tf_op jit(solution)/shard_map/ppermute | solution.py:30
  477.1 1.9 copy-start.2
  510.8 52.6 %copy-start.1 = (bf16[256,1536]{1,0:T(8,128)(2,1)S(1)}, bf16[256,1536]{1,0:T(8,128)(2,1)}, u32[]{:S(2)}) copy-start(bf16[256,1536]{1,0:T(8,128)(2,1)} %param.7) | copy-start | bytes 2359300
Sparse Core Ops, SparseCore 0:
  111.5 179.9 all-gather.1
